TPU v7x, 32 devices: a whole 2x2x4 slice. The times are simulated.
32 devices in a mesh: seq: 8 (over z, x), head: 4 (over y, core).
Axes of the slice: x: 2, y: 2, z: 4, core: 2. Of those that a mesh axis runs over, the one named last changes fastest.
Arguments:
- tokens: bfloat16 [1024, 2048], P('seq', 'head'), may hold values from -6 to 6
- norm_gain: float32 [2048], replicated, may hold values from 0.1 to 1.9
- query_weight: bfloat16 [2048, 2048], P(None, 'head')
- key_weight: bfloat16 [2048, 256], replicated, may hold values from -0.125 to 0.125
- value_weight: bfloat16 [2048, 256], replicated, may hold values from -0.125 to 0.125
- window_lengths: int32 [8], replicated, may hold values from 1 to 256, 1024 in all
- is_caption: int32 [1024], P('seq'), may hold values 0 or 1
- span_blocks: int32 [8, 2], P('seq'), may hold values from 0 to 7, as said below
Outputs:
- attended: bfloat16 [1024, 2048], P('seq', 'head')
Inputs may be any that keep to these rules, and one draw needn't show every extreme that they name: `window_lengths`: window lengths are whole numbers summing to 1024, the largest exactly 256. `is_caption`: 1 marks a caption token, 0 a visual token. `span_blocks`: row b holds first and last key block of one event span: first <= last <= first + 1 and first <= 6; some span has exactly 2 blocks.
All inputs are finite; a program needn't handle non-finite values. No bound on the sum of `is_caption` on one device may be relied on, other than what follows from the above.
Results may differ from a plain program's by a relative error of at most 0.019.
The roundings to bfloat16 on the way count: a program that leaves them out, or rounds other values in their place, can miss the bound.
Values may be sent and summed in bfloat16 or wider, within the bound.
No kernel may reach another device: no remote copies, remote signals or barrier semaphores. Data moves between devices by JAX's collectives and lax.ppermute only.
A program may use at most 64 MiB of HBM per device.

v0:
```python
import jax
import jax.numpy as jnp
from jax import lax
from jax.sharding import PartitionSpec as P

H = 16
KV = 2
HD = 128
BLOCK = 128
norm_eps = 1e-05
rope_base = 500000.0
window_cap = 4096
span_cap = 8
slice_blocks = 8
lowest_start = -1e30


def rotate(vectors, position):
    half_size = vectors.shape[-1] // 2
    frequency = rope_base ** (-jnp.arange(half_size, dtype=jnp.float32) * 2.0 / vectors.shape[-1])
    angles = position.astype(jnp.float32)[:, None] * frequency[None, :]
    cosine = jnp.cos(angles)[:, None, :]
    sine_part = jnp.sin(angles)[:, None, :]
    first_half = vectors[..., :half_size]
    second_half = vectors[..., half_size:]
    return jnp.concatenate(
        [
            first_half * cosine - second_half * sine_part,
            second_half * cosine + first_half * sine_part,
        ],
        -1,
    )


def rms_normed(tokens, norm_gain):
    hidden = tokens.astype(jnp.float32)
    scale = lax.rsqrt(jnp.mean(hidden * hidden, -1, keepdims=True) + norm_eps)
    return (hidden * scale * norm_gain[None, :]).astype(jnp.bfloat16)


def window_starts(window_lengths, position):
    window_ends = jnp.cumsum(window_lengths)
    begins = window_ends - window_lengths
    within = (begins[None, :] <= position[:, None]) & (position[:, None] < window_ends[None, :])
    return jnp.sum(jnp.where(within, begins[None, :], 0), 1)


def inside(first_row, row_pos, key_pos):
    return (first_row[:, None] <= key_pos[None, :]) & (key_pos[None, :] <= row_pos[:, None])


def absorb(softmax_state, queries, key_values, allowed):
    highest, denominator, weighted = softmax_state
    head_size = queries.shape[-1]
    scores = jnp.einsum(
        "rhd,nd->rhn", queries, key_values[:, :head_size], preferred_element_type=jnp.float32
    )
    scores = jnp.where(allowed[:, None, :], scores, -jnp.inf)
    updated = jnp.maximum(highest, jnp.max(scores, -1))
    rescale = jnp.exp(highest - updated)
    weights = jnp.exp(scores - updated[..., None])
    denominator = rescale * denominator + jnp.sum(weights, -1)
    weighted = rescale[..., None] * weighted + jnp.einsum(
        "rhn,nd->rhd",
        weights.astype(jnp.bfloat16),
        key_values[:, head_size:],
        preferred_element_type=jnp.float32,
    )
    return (updated, denominator, weighted)


def absorb_sliced(softmax_state, queries, key_values, allowed):
    key_count = key_values.shape[0]
    piece = slice_blocks * BLOCK
    for begin in range(0, key_count, piece):
        finish = min(begin + piece, key_count)
        softmax_state = absorb(
            softmax_state, queries, key_values[begin:finish], allowed[:, begin:finish]
        )
    return softmax_state


def select(layout, wanted, total_blocks):
    blocks_dev = layout.shape[0]
    clipped = jnp.clip(wanted, 0, total_blocks - 1)
    return layout[clipped % blocks_dev, clipped // blocks_dev]


def per_device(
    tokens,
    norm_gain,
    query_weight,
    key_weight,
    value_weight,
    window_lengths,
    is_caption,
    span_blocks,
):
    ranks = lax.axis_size("seq")
    device_rank = lax.axis_index("seq")
    features = lax.all_gather(tokens, "head", axis=1, tiled=True)
    local_rows = features.shape[0]
    blocks_dev = local_rows // BLOCK
    total_blocks = blocks_dev * ranks
    window = min(window_cap, total_blocks * BLOCK // 4)
    span_most = min(span_cap, total_blocks // 4)
    window_back = (window + BLOCK - 2) // BLOCK
    first_pos = device_rank * local_rows
    row_pos = first_pos + jnp.arange(local_rows, dtype=jnp.int32)
    normed = rms_normed(features, norm_gain)
    head_dev = query_weight.shape[1] // HD
    kv_index = lax.axis_index("head") * head_dev // (H // KV)
    queries = jnp.dot(normed, query_weight, preferred_element_type=jnp.float32).reshape(
        local_rows, head_dev, HD
    )
    queries = (rotate(queries, row_pos) * HD ** (-0.5)).astype(jnp.bfloat16)
    key_columns = lax.dynamic_slice_in_dim(key_weight, kv_index * HD, HD, 1)
    value_columns = lax.dynamic_slice_in_dim(value_weight, kv_index * HD, HD, 1)
    key_rows = jnp.dot(normed, key_columns, preferred_element_type=jnp.float32).reshape(
        local_rows, 1, HD
    )
    key_rows = rotate(key_rows, row_pos).reshape(local_rows, HD).astype(jnp.bfloat16)
    value_rows = jnp.dot(normed, value_columns, preferred_element_type=jnp.float32).astype(
        jnp.bfloat16
    )
    key_values = jnp.concatenate([key_rows, value_rows], 1)
    window_first = window_starts(window_lengths, row_pos)
    caption_rows = is_caption == 1
    row_block = jnp.arange(local_rows, dtype=jnp.int32) // BLOCK
    span_end = span_blocks[:, 1][row_block]
    all_spans = lax.all_gather(span_blocks, "seq", axis=0, tiled=True)
    pieces = key_values.reshape(blocks_dev, ranks, BLOCK // ranks, 2 * HD)
    layout = lax.all_to_all(pieces, "seq", split_axis=1, concat_axis=1, tiled=True)
    offsets = jnp.arange(span_most, dtype=jnp.int32)
    span_wanted = all_spans[:, 0].reshape(ranks, blocks_dev, 1) + offsets[None, None, :]
    span_wanted = span_wanted.reshape(ranks, blocks_dev * span_most).T
    own_starts = span_blocks[:, 0]
    span_pos = (
        (own_starts[:, None] + offsets[None, :])[:, :, None] * BLOCK
        + jnp.arange(BLOCK, dtype=jnp.int32)[None, None, :]
    ).reshape(-1)
    span_owner = jnp.arange(blocks_dev * span_most * BLOCK, dtype=jnp.int32) // (span_most * BLOCK)
    span_ok = (span_owner[None, :] == row_block[:, None]) & (
        span_pos[None, :] // BLOCK <= span_end[:, None]
    )
    span_ok = span_ok & caption_rows[:, None] & ~inside(window_first, row_pos, span_pos)
    start_state = (
        jnp.full((local_rows, head_dev), lowest_start, jnp.float32),
        jnp.zeros((local_rows, head_dev), jnp.float32),
        jnp.zeros((local_rows, head_dev, HD), jnp.float32),
    )
    near_index = jnp.arange(window_back + blocks_dev, dtype=jnp.int32)
    near_wanted = (
        (jnp.arange(ranks, dtype=jnp.int32) * blocks_dev)[None, :]
        - window_back
        + near_index[:, None]
    )
    wanted = jnp.concatenate([near_wanted, span_wanted], 0)
    delivered = lax.all_to_all(
        select(layout, wanted, total_blocks), "seq", split_axis=1, concat_axis=1, tiled=True
    )
    gathered = delivered.reshape(-1, 2 * HD)
    near_pos = (first_pos // BLOCK - window_back) * BLOCK + jnp.arange(
        (window_back + blocks_dev) * BLOCK, dtype=jnp.int32
    )
    allowed = jnp.concatenate([inside(window_first, row_pos, near_pos), span_ok], 1)
    softmax_state = absorb_sliced(start_state, queries, gathered, allowed)
    highest, denominator, weighted = softmax_state
    return (
        (weighted / denominator[..., None]).reshape(local_rows, head_dev * HD).astype(jnp.bfloat16)
    )


def solution(mesh):
    in_specs = (P("seq", "head"), P(), P(None, "head"), P(), P(), P(), P("seq"), P("seq", None))
    out_specs = P("seq", "head")
    return jax.shard_map(
        per_device, mesh=mesh, in_specs=in_specs, out_specs=out_specs, check_vma=False
    )
```

profile of v0, /device:TPU:0, one launch (start us, length us, event | category | flops | bytes accessed | tf_op | source)
XLA Modules:
  0.0 59.4 jit_solution(15557514870400121325)
XLA Ops:
  0.0 0.0 copy-start
  0.0 0.0 copy-start.1
  0.1 9.0 %all_gather.6 = bf16[128,2048]{1,0:T(8,128)(2,1)S(1)} all-gather(bf16[128,512]{1,0:T(8,128)(2,1)} %param.8), channel_id=1, replica_groups=mesh['seq'=8,'head'=4] {'head'}, dimensions={1}, use_global_device_ids=true | all-gather | bytes 655360 | tf_op jit(solution)/shard_map/all_gather | solution.py:101
  9.1 0.2 fusion.4
  9.3 0.0 copy-start.3
  9.3 0.0 copy-start.4
  9.3 0.0 copy-start.2
  9.3 1.5 %convolution_convert_fusion = bf16[128,128]{0,1:T(8,128)(2,1)S(1)} fusion(bf16[2048,256]{1,0:T(8,128)(2,1)} %param.12, s32[]{:T(128)S(6)} %select_n.76, bf16[128,2048]{1,0:T(8,128)(2,1)S(1)} %all_gather.6, f32[2048]{0:T(1024)} %param.9, f32[128]{0:T(128)S(1)} %add_rsqrt_fusion), kind=kOutput, calls=%fused_computation.11 | convolution fusion | flops 68173824 | bytes 1090052 | tf_op jit(solution)/shard_map/dot_general | solution.py:123
  10.8 0.0 copy-done.1
  10.8 1.5 %convolution_bitcast_fusion = f32[128,1,128]{0,2,1:T(8,128)S(1)} fusion(bf16[2048,256]{1,0:T(8,128)(2,1)} %param.11, s32[]{:T(128)S(6)} %select_n.76, bf16[128,2048]{1,0:T(8,128)(2,1)S(1)} %all_gather.6, f32[2048]{0:T(1024)S(1)} %copy-done.1, f32[128]{0:T(128)S(1)} %add_rsqrt_fusion), kind=kOutput, calls=%fused_computation.10 | convolution fusion | flops 68157440 | bytes 1122820 | tf_op jit(solution)/shard_map/dot_general | solution.py:119
  12.3 0.2 fusion.19
  12.5 0.7 %copy.33 = bf16[128,256]{1,0:T(8,128)(2,1)} copy(bf16[128,256]{0,1:T(8,128)(2,1)S(1)} %pad_maximum_fusion) | data formatting | bytes 131072 | tf_op jit(solution)/shard_map/concatenate | solution.py:126
  13.2 5.8 %all-to-all-start = ((bf16[1,8,16,256]{3,2,0,1:T(8,128)(2,1)}), bf16[1,8,16,256]{3,2,0,1:T(8,128)(2,1)S(1)}, u32[]{:S(2)}, u32[]{:S(2)}) async-start(bf16[1,8,16,256]{3,2,0,1:T(8,128)(2,1)} %bitcast.9), calls=%async_computation | async-start | bytes 131072 | tf_op jit(solution)/shard_map/all_to_all | solution.py:133
  19.1 0.3 multiply_cosine_fusion
  19.4 0.0 copy-done.3
  19.4 0.2 reduce-window.8
  19.6 0.0 copy-done.4
  19.6 0.0 copy-done.2
  19.6 0.6 %fusion.36 = (s32[1,1]{1,0:T(1,128)}, s32[1,1]{1,0:T(1,128)}) fusion(s32[1,2]{1,0:T(1,128)S(1)} %copy-done.2), kind=kLoop, calls=%fused_computation.82 | loop fusion | bytes 16 | tf_op jit(solution)/shard_map/slice | solution.py:130
  20.2 0.6 %add_multiply_fusion = s32[2]{0:T(128)S(1)} fusion(s32[]{:T(128)} %bitcast.2), kind=kLoop, calls=%fused_computation.70 | loop fusion | flops 4 | bytes 12 | tf_op jit(solution)/shard_map/mul | solution.py:139
  20.8 0.1 add.213
  20.9 0.6 %fusion.24 = pred[256]{0:T(512)(128)(4,1)S(1)} fusion(s32[]{:T(128)} %bitcast.5, s32[256]{0:T(256)S(1)} %bitcast.47), kind=kLoop, calls=%fused_computation.65 | loop fusion | flops 4352 | bytes 1284 | tf_op jit(solution)/shard_map/le | solution.py:144
  21.6 21.0 %all-gather = s32[8,1,2]{2,1,0:T(1,128)S(1)} all-gather(s32[1,1,2]{2,1,0:T(1,128)S(1)} %bitcast.45), channel_id=1, replica_groups=mesh['seq'=8,'head'=4] {'seq'}, dimensions={0}, use_global_device_ids=true | all-gather | bytes 72 | tf_op jit(solution)/shard_map/all_gather | solution.py:131
  42.5 0.1 copy.35
  42.7 0.1 reshape.403
  42.7 0.0 copy-done
  42.7 0.5 fusion.33
  43.2 0.1 reshape.399
  43.3 0.1 select_reduce_fusion
  43.4 0.1 compare_and_fusion
  43.6 0.1 not_and_fusion
  43.7 0.0 all-to-all-done
  43.7 0.6 %gather_fusion = bf16[40,16,256]{2,1,0:T(8,128)(2,1)S(1)} fusion(bf16[1,8,16,256]{3,2,1,0:T(8,128)(2,1)S(1)} %bitcast.40, s32[40]{0:T(128)S(1)} %reshape.403), kind=kCustom, calls=%fused_computation | custom fusion | bytes 655680 | tf_op jit(solution)/shard_map/gather | solution.py:86
  44.3 0.7 %copy.37 = bf16[5,8,16,256]{3,2,0,1:T(8,128)(2,1)} copy(bf16[5,8,16,256]{3,2,1,0:T(8,128)(2,1)S(1)} %bitcast.41) | data formatting | bytes 655360 | tf_op jit(solution)/shard_map/gather | solution.py:86
  45.1 3.4 %all-to-all-start.1 = ((bf16[5,8,16,256]{3,2,0,1:T(8,128)(2,1)}), bf16[5,8,16,256]{3,2,0,1:T(8,128)(2,1)S(1)}, u32[]{:S(2)}, u32[]{:S(2)}) async-start(bf16[5,8,16,256]{3,2,0,1:T(8,128)(2,1)} %copy.37), calls=%async_computation.1 | async-start | bytes 655360 | tf_op jit(solution)/shard_map/all_to_all | solution.py:159
  48.6 0.2 fusion.35
  48.8 0.1 multiply_subtract_fusion
  48.8 8.3 %all-to-all-done.1 = bf16[5,8,16,256]{3,2,0,1:T(8,128)(2,1)S(1)} async-done(((bf16[5,8,16,256]{3,2,0,1:T(8,128)(2,1)}), bf16[5,8,16,256]{3,2,0,1:T(8,128)(2,1)S(1)}, u32[]{:S(2)}, u32[]{:S(2)}) %all-to-all-start.1) | async-done | bytes 327712 | tf_op jit(solution)/shard_map/all_to_all | solution.py:159
  57.2 0.5 fusion.37
  57.7 0.4 fusion.1
  58.1 0.5 fusion.3
  58.6 0.8 %copy.40 = bf16[128,512]{1,0:T(8,128)(2,1)} copy(bf16[128,512]{0,1:T(8,128)(2,1)S(1)} %bitcast.44) | data formatting | bytes 262144 | tf_op jit(solution)/shard_map/convert_element_type | solution.py:170
  (19 shorter events, 0.2 us)
Async XLA Ops:
  0.0 42.7 %copy-start = (bf16[2048,512]{1,0:T(8,128)(2,1)S(1)}, bf16[2048,512]{1,0:T(8,128)(2,1)}, u32[]{:S(2)}) copy-start(bf16[2048,512]{1,0:T(8,128)(2,1)} %param.10) | copy-start | bytes 6291460
  0.0 10.8 %copy-start.1 = (f32[2048]{0:T(1024)S(1)}, f32[2048]{0:T(1024)}, u32[]{:S(2)}) copy-start(f32[2048]{0:T(1024)} %param.9) | copy-start | bytes 24580
  9.3 10.1 %copy-start.3 = (s32[8]{0:T(128)S(1)}, s32[8]{0:T(128)}, u32[]{:S(2)}) copy-start(s32[8]{0:T(128)} %param.13) | copy-start | bytes 100
  9.3 10.3 %copy-start.4 = (s32[128]{0:T(128)S(1)}, s32[128]{0:T(128)}, u32[]{:S(2)}) copy-start(s32[128]{0:T(128)} %param.14) | copy-start | bytes 1540
  9.3 10.3 %copy-start.2 = (s32[1,2]{1,0:T(1,128)S(1)}, s32[1,2]{1,0:T(1,128)}, u32[]{:S(2)}) copy-start(s32[1,2]{1,0:T(1,128)} %param.15) | copy-start | bytes 28
  13.2 30.5 %all-to-all-start = ((bf16[1,8,16,256]{3,2,0,1:T(8,128)(2,1)}), bf16[1,8,16,256]{3,2,0,1:T(8,128)(2,1)S(1)}, u32[]{:S(2)}, u32[]{:S(2)}) async-start(bf16[1,8,16,256]{3,2,0,1:T(8,128)(2,1)} %bitcast.9), calls=%async_computation | async-start | bytes 131072 | tf_op jit(solution)/shard_map/all_to_all | solution.py:133
  45.1 12.0 %all-to-all-start.1 = ((bf16[5,8,16,256]{3,2,0,1:T(8,128)(2,1)}), bf16[5,8,16,256]{3,2,0,1:T(8,128)(2,1)S(1)}, u32[]{:S(2)}, u32[]{:S(2)}) async-start(bf16[5,8,16,256]{3,2,0,1:T(8,128)(2,1)} %copy.37), calls=%async_computation.1 | async-start | bytes 655360 | tf_op jit(solution)/shard_map/all_to_all | solution.py:159
where the time goes:
time: 59.8 us; the launch traced here: 59.4 us
  blocking collectives  30 us (50%)
  starting transfers between devices  9.23 us (15%)
  waiting for transfers between devices  8.3 us (14%)
  matrix products  4.45 us (7%)
  local copies, waits for them, and re-layouts  4.08 us (7%)
  other arithmetic  3.04 us (5%)
    all_gather x1, blocking collectives, per_device(): all_spans = lax.all_gather(span_blocks, 'seq', axis=0, tiled=True)  21 us
    all_gather x1, blocking collectives, per_device(): features = lax.all_gather(tokens, 'head', axis=1, tiled=True)  9.02 us
    all_to_all x1, waiting for transfers between devices, per_device(): lax.all_to_all(select(layout, wanted, total_blocks), 'seq', split_axis=1,...  8.3 us
    all_to_all x1, starting transfers between devices, per_device(): lax.all_to_all(pieces, 'seq', split_axis=1, concat_axis=1, tiled=True)  5.8 us
    all_to_all x1, starting transfers between devices, per_device(): lax.all_to_all(select(layout, wanted, total_blocks), 'seq', split_axis=1,...  3.43 us
    dot_general x1, matrix products, per_device(): jnp.dot(normed, value_columns, preferred_element_type=jnp.float32)  1.48 us
    dot_general x1, matrix products, per_device(): jnp.dot(normed, key_columns, preferred_element_type=jnp.float32)  1.45 us
    gather x2, local copies, waits for them, and re-layouts, select(): return layout[clipped % blocks_dev, clipped // blocks_dev]  1.37 us
  transfers between devices with their start and end apart: 2, of which 1 were waited for; matrix products, arithmetic and copies ran while one was open for 6% of the time, Pallas kernels for 0%

commit v1 on v0

--- a/solution.py
+++ b/solution.py
@@ -13,6 +13,15 @@
 span_cap = 8
 slice_blocks = 8
 lowest_start = -1e30
+touch_local_data = lambda u_in, comm_axis, pos_dim, axis_k: jnp.concatenate(
+    lax.all_to_all(
+        jnp.stack(jnp.split(u_in, lax.axis_size(comm_axis), pos_dim), 0),
+        axis_name=comm_axis,
+        split_axis=0,
+        concat_axis=0,
+    ),
+    axis=axis_k,
+)
 
 
 def rotate(vectors, position):
@@ -156,9 +165,7 @@
         + near_index[:, None]
     )
     wanted = jnp.concatenate([near_wanted, span_wanted], 0)
-    delivered = lax.all_to_all(
-        select(layout, wanted, total_blocks), "seq", split_axis=1, concat_axis=1, tiled=True
-    )
+    delivered = touch_local_data(select(layout, wanted, total_blocks), "seq", 1, 1)
     gathered = delivered.reshape(-1, 2 * HD)
     near_pos = (first_pos // BLOCK - window_back) * BLOCK + jnp.arange(
         (window_back + blocks_dev) * BLOCK, dtype=jnp.int32

time: 59.8 us -> 64 us (1.070)
  local copies, waits for them, and re-layouts: 4.08 us -> 8.26 us
    unnamed x10 -> x17, local copies, waits for them, and re-layouts: 0.03 us -> 4.34 us
    gather x2 -> x1, local copies, waits for them, and re-layouts: 1.37 us -> 0.63 us  [select(): return layout[clipped % blocks_dev, clipped // blocks_dev]]
where the time goes in v1:
time: 64 us; the launch traced here: 63.6 us
  blocking collectives  30 us (47%)
  starting transfers between devices  9.23 us (14%)
  waiting for transfers between devices  8.3 us (13%)
  local copies, waits for them, and re-layouts  8.26 us (13%)
  matrix products  4.46 us (7%)
  other arithmetic  3.04 us (5%)
    all_gather x1, blocking collectives, per_device(): all_spans = lax.all_gather(span_blocks, 'seq', axis=0, tiled=True)  21 us
    all_gather x1, blocking collectives, per_device(): features = lax.all_gather(tokens, 'head', axis=1, tiled=True)  9.02 us
    all_to_all x1, waiting for transfers between devices, lax.all_to_all(jnp.stack(jnp.split(u_in, lax.axis_size(comm_axis), pos_di...  8.3 us
    all_to_all x1, starting transfers between devices, per_device(): lax.all_to_all(pieces, 'seq', split_axis=1, concat_axis=1, tiled=True)  5.8 us
    unnamed x17, local copies, waits for them, and re-layouts  4.34 us
    all_to_all x1, starting transfers between devices, lax.all_to_all(jnp.stack(jnp.split(u_in, lax.axis_size(comm_axis), pos_di...  3.43 us
    dot_general x1, matrix products, per_device(): jnp.dot(normed, value_columns, preferred_element_type=jnp.float32)  1.48 us
    dot_general x1, matrix products, per_device(): jnp.dot(normed, key_columns, preferred_element_type=jnp.float32)  1.45 us
  transfers between devices with their start and end apart: 2, of which 1 were waited for; matrix products, arithmetic and copies ran while one was open for 6% of the time, Pallas kernels for 0%

profile of v1, /device:TPU:0, one launch (start us, length us, event | category | flops | bytes accessed | tf_op | source)
XLA Modules:
  0.0 63.6 jit_solution(134616481280322877)
XLA Ops:
  0.0 0.0 copy-start
  0.1 9.0 %all_gather.6 = bf16[128,2048]{1,0:T(8,128)(2,1)S(1)} all-gather(bf16[128,512]{1,0:T(8,128)(2,1)} %param.8), channel_id=1, replica_groups=mesh['seq'=8,'head'=4] {'head'}, dimensions={1}, use_global_device_ids=true | all-gather | bytes 655360 | tf_op jit(solution)/shard_map/all_gather | solution.py:110
  9.1 0.2 fusion.4
  9.3 0.0 copy-start.3
  9.3 0.0 copy-start.4
  9.3 0.0 copy-start.2
  9.3 1.5 %convolution_convert_fusion = bf16[128,128]{0,1:T(8,128)(2,1)S(1)} fusion(bf16[2048,256]{1,0:T(8,128)(2,1)} %param.12, s32[]{:T(128)S(6)} %select_n.76, bf16[128,2048]{1,0:T(8,128)(2,1)S(1)} %all_gather.6, f32[2048]{0:T(1024)} %param.9, f32[128]{0:T(128)S(1)} %add_rsqrt_fusion), kind=kOutput, calls=%fused_computation.11 | convolution fusion | flops 68173824 | bytes 1090052 | tf_op jit(solution)/shard_map/dot_general | solution.py:132
  10.8 0.0 copy-done.1
  10.8 1.5 %convolution_bitcast_fusion = f32[128,1,128]{0,2,1:T(8,128)S(1)} fusion(bf16[2048,256]{1,0:T(8,128)(2,1)} %param.11, s32[]{:T(128)S(6)} %select_n.76, bf16[128,2048]{1,0:T(8,128)(2,1)S(1)} %all_gather.6, f32[2048]{0:T(1024)S(1)} %copy-done.1, f32[128]{0:T(128)S(1)} %add_rsqrt_fusion), kind=kOutput, calls=%fused_computation.10 | convolution fusion | flops 68157440 | bytes 1122820 | tf_op jit(solution)/shard_map/dot_general | solution.py:128
  12.3 0.2 fusion.27
  12.5 0.7 %copy.55 = bf16[128,256]{1,0:T(8,128)(2,1)} copy(bf16[128,256]{0,1:T(8,128)(2,1)S(1)} %pad_maximum_fusion) | data formatting | bytes 131072 | tf_op jit(solution)/shard_map/concatenate | solution.py:135
  13.2 5.8 %all-to-all-start = ((bf16[1,8,16,256]{3,2,0,1:T(8,128)(2,1)}), bf16[1,8,16,256]{3,2,0,1:T(8,128)(2,1)S(1)}, u32[]{:S(2)}, u32[]{:S(2)}) async-start(bf16[1,8,16,256]{3,2,0,1:T(8,128)(2,1)} %bitcast.9), calls=%async_computation | async-start | bytes 131072 | tf_op jit(solution)/shard_map/all_to_all | solution.py:142
  19.1 0.3 multiply_cosine_fusion
  19.4 0.0 copy-done.3
  19.4 0.2 reduce-window.8
  19.6 0.0 copy-done.4
  19.6 0.0 copy-done.2
  19.6 0.6 fusion.44
  20.2 0.6 add_multiply_fusion
  20.8 0.1 add.213
  20.9 0.6 fusion.32
  21.6 21.0 %all-gather = s32[8,1,2]{2,1,0:T(1,128)S(1)} all-gather(s32[1,1,2]{2,1,0:T(1,128)S(1)} %bitcast.102), channel_id=1, replica_groups=mesh['seq'=8,'head'=4] {'seq'}, dimensions={0}, use_global_device_ids=true | all-gather | bytes 72 | tf_op jit(solution)/shard_map/all_gather | solution.py:140
  42.5 0.1 copy.57
  42.7 0.1 reshape.403
  42.7 0.0 copy-done
  42.7 0.5 fusion.41
  43.2 0.1 reshape.399
  43.3 0.1 select_reduce_fusion
  43.4 0.1 compare_and_fusion
  43.6 0.1 not_and_fusion
  43.7 0.0 all-to-all-done
  43.7 0.6 gather_fusion
  44.3 0.6 fusion.25
  45.0 0.6 fusion.24
  45.6 0.6 fusion.23
  46.2 0.6 fusion.22
  46.8 0.6 fusion.21
  47.4 0.6 fusion.20
  48.0 0.6 fusion.19
  48.7 0.6 fusion.18
  49.3 3.4 %all-to-all-start.1 = ((bf16[8,5,1,16,256]{4,3,1,2,0:T(8,128)(2,1)}), bf16[8,5,1,16,256]{4,3,1,2,0:T(8,128)(2,1)S(1)}, u32[]{:S(2)}, u32[]{:S(2)}) async-start(bf16[8,5,1,16,256]{4,3,1,2,0:T(8,128)(2,1)} %fusion.18), calls=%async_computation.1 | async-start | bytes 655360 | tf_op jit(solution)/shard_map/all_to_all | solution.py:17
  52.7 0.2 fusion.43
  52.9 0.1 multiply_subtract_fusion
  53.0 8.3 %all-to-all-done.1 = bf16[8,5,1,16,256]{4,3,1,2,0:T(8,128)(2,1)S(1)} async-done(((bf16[8,5,1,16,256]{4,3,1,2,0:T(8,128)(2,1)}), bf16[8,5,1,16,256]{4,3,1,2,0:T(8,128)(2,1)S(1)}, u32[]{:S(2)}, u32[]{:S(2)}) %all-to-all-start.1) | async-done | bytes 327712 | tf_op jit(solution)/shard_map/all_to_all | solution.py:17
  61.3 0.5 fusion.45
  61.8 0.4 fusion.1
  62.3 0.5 fusion.3
  62.8 0.8 %copy.69 = bf16[128,512]{1,0:T(8,128)(2,1)} copy(bf16[128,512]{0,1:T(8,128)(2,1)S(1)} %bitcast.101) | data formatting | bytes 262144 | tf_op jit(solution)/shard_map/convert_element_type | solution.py:177
  (20 shorter events, 0.2 us)
Async XLA Ops:
  0.0 42.7 %copy-start = (bf16[2048,512]{1,0:T(8,128)(2,1)S(1)}, bf16[2048,512]{1,0:T(8,128)(2,1)}, u32[]{:S(2)}) copy-start(bf16[2048,512]{1,0:T(8,128)(2,1)} %param.10) | copy-start | bytes 6291460
  0.0 10.8 %copy-start.1 = (f32[2048]{0:T(1024)S(1)}, f32[2048]{0:T(1024)}, u32[]{:S(2)}) copy-start(f32[2048]{0:T(1024)} %param.9) | copy-start | bytes 24580
  9.3 10.1 %copy-start.3 = (s32[8]{0:T(128)S(1)}, s32[8]{0:T(128)}, u32[]{:S(2)}) copy-start(s32[8]{0:T(128)} %param.13) | copy-start | bytes 100
  9.3 10.3 %copy-start.4 = (s32[128]{0:T(128)S(1)}, s32[128]{0:T(128)}, u32[]{:S(2)}) copy-start(s32[128]{0:T(128)} %param.14) | copy-start | bytes 1540
  9.3 10.3 %copy-start.2 = (s32[1,2]{1,0:T(1,128)S(1)}, s32[1,2]{1,0:T(1,128)}, u32[]{:S(2)}) copy-start(s32[1,2]{1,0:T(1,128)} %param.15) | copy-start | bytes 28
  13.2 30.5 %all-to-all-start = ((bf16[1,8,16,256]{3,2,0,1:T(8,128)(2,1)}), bf16[1,8,16,256]{3,2,0,1:T(8,128)(2,1)S(1)}, u32[]{:S(2)}, u32[]{:S(2)}) async-start(bf16[1,8,16,256]{3,2,0,1:T(8,128)(2,1)} %bitcast.9), calls=%async_computation | async-start | bytes 131072 | tf_op jit(solution)/shard_map/all_to_all | solution.py:142
  49.3 12.0 %all-to-all-start.1 = ((bf16[8,5,1,16,256]{4,3,1,2,0:T(8,128)(2,1)}), bf16[8,5,1,16,256]{4,3,1,2,0:T(8,128)(2,1)S(1)}, u32[]{:S(2)}, u32[]{:S(2)}) async-start(bf16[8,5,1,16,256]{4,3,1,2,0:T(8,128)(2,1)} %fusion.18), calls=%async_computation.1 | async-start | bytes 655360 | tf_op jit(solution)/shard_map/all_to_all | solution.py:17
